TPU v7x, 512 devices: a whole 4x8x8 slice. The times are simulated.
512 devices in a mesh: dom: 32 (over x, y_hi, core), bucket: 8 (over z), depth: 2 (over y_lo).
Axes of the slice: x: 4, y: 8 (y_hi: 4, y_lo: 2; y = y_hi * 2 + y_lo), z: 8, core: 2. Of those that a mesh axis runs over, the one named last changes fastest.
Arguments:
- entities: float32 [262144, 400], P(('dom', 'bucket')), may hold values from -7 to 7
- entity_state: float32 [262144], P(('dom', 'bucket')), may hold values from 0.05 to 0.5
- relations: float32 [256, 400], replicated, may hold values from 0.5 to 2
- relation_state: float32 [256], replicated, may hold values from 0.05 to 0.5
- edge_ends: int32 [2, 262144], P(None, ('dom', 'bucket')), may hold values from 0 to 1023
- relation_ids: int32 [262144], P(('dom', 'bucket')), may hold values from 0 to 255
- neg_ids: int32 [512, 1024], P(('dom', 'bucket'), 'depth'), may hold values from 0 to 1023
- edge_count: int32 [256], P(('dom', 'bucket')), may hold values from 16 to 1024, as said below
Outputs:
- new_entities: float32 [262144, 400], P(('dom', 'bucket'))
- new_state: float32 [262144], P(('dom', 'bucket'))
- new_relations: float32 [256, 400], replicated
Inputs may be any that keep to these rules, and one draw needn't show every extreme that they name: `edge_count`: the live slots of a partition are its first ones; partition 0 is full in every draw.
All inputs are finite; a program needn't handle non-finite values.
Results may differ from a plain program's by a relative error of at most 0.0006.
The roundings to bfloat16 on the way count: a program that leaves them out, or rounds other values in their place, can miss the bound.
Values may be sent and summed in bfloat16 or wider, within the bound.
No kernel may reach another device: no remote copies, remote signals or barrier semaphores. Data moves between devices by JAX's collectives and lax.ppermute only.
A program may use at most 64 MiB of HBM per device.

v0:
```python
import jax
import jax.numpy as jnp
from jax import lax
from jax.sharding import PartitionSpec as P

BLOCK = 512


entity_rate = 0.1
relation_rate = 1.0


def passed_along(block, axis, distance):
    devices = range(lax.axis_size(axis))
    route = [((i - distance) % len(devices), i) for i in devices]
    return lax.ppermute(block, axis, route)


def merged(value, axis, join):
    pieces = jax.tree.map(lambda part: lax.all_gather(part, axis), value)
    head = jax.tree.map(lambda part: part[0], pieces)
    tail = jax.tree.map(lambda part: part[1:], pieces)
    total, _ = lax.scan(lambda total, share: (join(total, share), None), head, tail)
    return total


def merge_totals(earlier, later):
    peak = jnp.maximum(earlier[0], later[0])
    return (peak, earlier[1] * jnp.exp(earlier[0] - peak) + later[1] * jnp.exp(later[0] - peak))


def adagrad_rows(values, state, grad):
    updated = state + jnp.mean(grad * grad, axis=1)
    return (values - entity_rate * grad / jnp.sqrt(updated)[:, None], updated)


def pick_rows(table, row_ids):
    columns = jnp.arange(table.shape[0], dtype=jnp.int32)
    selector = (row_ids[:, None] == columns[None, :]).astype(jnp.bfloat16)
    return jnp.dot(selector, table, preferred_element_type=jnp.float32).astype(jnp.bfloat16)


def local(
    entities, entity_state, relations, relation_state, edge_ends, relation_ids, neg_ids, edge_count
):
    half_dom = lax.axis_size("dom") // 2
    own_rows = entities.astype(jnp.bfloat16)
    far_rows = passed_along(own_rows, "dom", half_dom)
    live_count = edge_count[0]
    offsets = jnp.arange(BLOCK, dtype=jnp.int32)

    def block_inputs(block_index):
        first_slot = (block_index * BLOCK).astype(jnp.int32)
        left_ids = lax.dynamic_slice_in_dim(edge_ends[0], first_slot, BLOCK)
        right_ids = lax.dynamic_slice_in_dim(edge_ends[1], first_slot, BLOCK)
        rel_ids = lax.dynamic_slice_in_dim(relation_ids, first_slot, BLOCK)
        negative_ids = lax.dynamic_index_in_dim(neg_ids, block_index, 0, keepdims=False)
        active = (first_slot + offsets < live_count).astype(jnp.float32)
        return (first_slot, left_ids, right_ids, rel_ids, negative_ids, active)

    def score_part(left_ids, right_ids, rel_ids, negative_ids):
        left_rows = pick_rows(own_rows, left_ids)
        right_rows = pick_rows(far_rows, right_ids)
        scaling = relations[rel_ids]
        queries = (left_rows.astype(jnp.float32) * scaling).astype(jnp.bfloat16)
        negatives = pick_rows(far_rows, negative_ids)
        positive = jnp.sum(queries.astype(jnp.float32) * right_rows.astype(jnp.float32), axis=1)
        scores = lax.dot_general(
            queries, negatives, (((1,), (1,)), ((), ())), preferred_element_type=jnp.float32
        )
        local_peak = jnp.max(scores, axis=1)
        shifted = jnp.exp(scores - local_peak[:, None])
        local_total = jnp.sum(shifted, axis=1)
        return (
            left_rows,
            right_rows,
            scaling,
            queries,
            negatives,
            positive,
            shifted,
            local_peak,
            local_total,
        )

    def grad_part(
        totals_in, parts, neg_peak, neg_total, left_ids, right_ids, rel_ids, negative_ids, active
    ):
        own_grad, far_grad, rel_grad = totals_in
        (
            left_rows,
            right_rows,
            scaling,
            queries,
            negatives,
            positive,
            shifted,
            local_peak,
            local_total,
        ) = parts
        peak = jnp.maximum(positive, neg_peak)
        denom = jnp.exp(positive - peak) + neg_total * jnp.exp(neg_peak - peak)
        weights = (shifted * (jnp.exp(local_peak - peak) * active / denom)[:, None]).astype(
            jnp.bfloat16
        )
        pos_coef = active * (jnp.exp(positive - peak) / denom - 1.0)
        half_coef = 0.5 * pos_coef
        query_grad = jnp.dot(weights, negatives, preferred_element_type=jnp.float32) + half_coef[
            :, None
        ] * right_rows.astype(jnp.float32)
        neg_grad = lax.dot_general(
            weights, queries, (((0,), (0,)), ((), ())), preferred_element_type=jnp.float32
        )
        own_grad = own_grad.at[left_ids].add(query_grad * scaling)
        far_grad = (
            far_grad.at[right_ids]
            .add(half_coef[:, None] * queries.astype(jnp.float32))
            .at[negative_ids]
            .add(neg_grad)
        )
        rel_grad = rel_grad.at[rel_ids].add(query_grad * left_rows.astype(jnp.float32))
        return (own_grad, far_grad, rel_grad)

    def one_block(block_index, totals_in):
        first_slot, left_ids, right_ids, rel_ids, negative_ids, active = block_inputs(block_index)
        parts = score_part(left_ids, right_ids, rel_ids, negative_ids)
        neg_peak, neg_total = merged((parts[7], parts[8]), "depth", merge_totals)
        return grad_part(
            totals_in,
            parts,
            neg_peak,
            neg_total,
            left_ids,
            right_ids,
            rel_ids,
            negative_ids,
            active,
        )

    zeros_rows = jnp.zeros(entities.shape, jnp.float32)
    start_totals = (zeros_rows, zeros_rows, jnp.zeros(relations.shape, jnp.float32))
    own_grad, far_grad, rel_grad = lax.fori_loop(0, neg_ids.shape[0], one_block, start_totals)
    rel_total = lax.psum(rel_grad, ("dom", "bucket", "depth"))
    rel_state = relation_state + jnp.mean(rel_total * rel_total, axis=1)
    new_relations = relations - relation_rate * rel_total / jnp.sqrt(rel_state)[:, None]
    summed_own, summed_far = lax.psum((own_grad, far_grad), "depth")
    home_grad = passed_along(summed_far, "dom", half_dom)
    new_entities, new_state = adagrad_rows(entities, entity_state, summed_own + home_grad)
    return (new_entities, new_state, new_relations)


def solution(mesh):
    return jax.shard_map(
        local,
        mesh=mesh,
        in_specs=(
            P(("dom", "bucket"), None),
            P(("dom", "bucket")),
            P(),
            P(),
            P(None, ("dom", "bucket")),
            P(("dom", "bucket")),
            P(("dom", "bucket"), "depth"),
            P(("dom", "bucket")),
        ),
        out_specs=(P(("dom", "bucket"), None), P(("dom", "bucket")), P()),
        check_vma=False,
    )
```

profile of v0, /device:TPU:1, one launch (start us, length us, event | category | flops | bytes accessed | tf_op | source)
XLA Modules:
  0.0 562.5 jit_solution(12763933654649712091)
XLA Ops:
  8.1 1.6 convert_element_type.98
  9.7 5.5 collective-permute-start
  15.1 1.3 copy.35
  16.6 13.1 %collective-permute-done = bf16[1024,400]{0,1:T(8,128)(2,1)S(1)} collective-permute-done((bf16[1024,400]{0,1:T(8,128)(2,1)S(1)}, bf16[1024,400]{0,1:T(8,128)(2,1)S(1)}, u32[]{:S(2)}, u32[]{:S(2)}) %collective-permute-start) | collective-permute-done | bytes 819232 | tf_op jit(solution)/shard_map/ppermute | solution.py:16
  29.7 1.3 copy.37
  31.0 1.6 broadcast_in_dim.52
  33.0 116.7 %while.31 = (s32[]{:T(128)}, f32[1024,400]{1,0:T(8,128)}, f32[1024,400]{1,0:T(8,128)S(1)}, f32[256,400]{1,0:T(8,128)S(1)}, s32[2,1024]{1,0:T(2,128)S(1)}, /*inde...) while((s32[]{:T(128)}, f32[1024,400]{1,0:T(8,128)}, ...), condition=%wide.region_8.9_spmd.clone, body=%wide.region_0.8_spmd.clone.sunk | while | flops 1895480832 | bytes 50795024 | solution.py:142
  33.6 2.9 fusion.55
  37.9 2.3 gather_fusion
  40.2 2.5 copy.46
  42.6 2.6 fusion.56
  47.2 6.3 %all-gather.8 = f32[2,1,512]{2,1,0:T(1,128)S(1)} all-gather(f32[1,1,512]{2,1,0:T(1,128)S(1)} %bitcast.68), channel_id=2, replica_groups=mesh['dom'=32,'bucket'=8,'depth'=2] {'depth'}, dimensions={0}, use_global_device_ids=true | all-gather | bytes 6144 | tf_op jit(solution)/shard_map/while/body/eval_jaxpr/all_gather | solution.py:20
  53.8 3.2 all-gather.9
  57.7 1.7 fusion.62
  59.4 2.5 copy.47
  61.9 7.1 %scatter_fusion = f32[1024,400]{1,0:T(8,128)} fusion(f32[1024,400]{1,0:T(8,128)} %get-tuple-element.551, s32[512]{0:T(512)} %bitcast.70, f32[512,400]{1,0:T(8,128)} %copy.47), kind=kCustom, calls=%fused_computation.1.clone.clone.1 | custom fusion | flops 204800 | bytes 2459648 | tf_op jit(solution)/shard_map/while/body/eval_jaxpr/scatter-add | solution.py:114
  69.0 1.7 convert_multiply_fusion.3
  70.7 2.5 copy.48
  73.2 5.0 scatter_fusion.1
  78.2 2.7 fusion.63
  80.9 5.0 scatter_fusion.2
  85.9 2.5 copy.49
  88.4 4.5 scatter_fusion.3
  93.5 2.9 fusion.55
  97.8 2.3 gather_fusion
  100.1 2.5 copy.46
  102.5 2.6 fusion.56
  107.1 3.2 all-gather.8
  110.5 3.2 all-gather.9
  114.5 1.7 fusion.62
  116.2 2.5 copy.47
  118.6 7.1 %scatter_fusion = f32[1024,400]{1,0:T(8,128)} fusion(f32[1024,400]{1,0:T(8,128)} %get-tuple-element.551, s32[512]{0:T(512)} %bitcast.70, f32[512,400]{1,0:T(8,128)} %copy.47), kind=kCustom, calls=%fused_computation.1.clone.clone.1 | custom fusion | flops 204800 | bytes 2459648 | tf_op jit(solution)/shard_map/while/body/eval_jaxpr/scatter-add | solution.py:114
  125.8 1.7 convert_multiply_fusion.3
  127.5 2.5 copy.48
  129.9 5.0 scatter_fusion.1
  135.0 2.7 fusion.63
  137.6 5.0 scatter_fusion.2
  142.7 2.5 copy.49
  145.1 4.5 scatter_fusion.3
  149.6 2.7 copy.38
  152.4 1.7 copy.39
  154.2 115.7 %all-reduce.6.cloned.1.call-done = (f32[1024,400]{0,1:T(8,128)}, f32[1024,400]{0,1:T(8,128)}) async-done(((f32[1024,400]{0,1:T(8,128)}, f32[1024,400]{0,1:T(8,128)}), (f32[1024,400]{0,1:T(8,128)}, f32[1024,400]{0,1:T(8,128)})) %all-reduce.6.cloned.1.call-update) | async-done | bytes 3276816 | tf_op jit(solution)/shard_map/psum | solution.py:146
  269.9 4.7 collective-permute-start.1
  275.6 270.9 %all-reduce.4.cloned.1.call-done = f32[256,400]{0,1:T(8,128)} async-done(((f32[256,400]{0,1:T(8,128)}), f32[256,400]{0,1:T(8,128)}) %all-reduce.4.cloned.1.call-update) | async-done | bytes 409616 | tf_op jit(solution)/shard_map/psum | solution.py:143
  546.5 1.1 multiply_reduce_fusion.1
  547.6 1.9 divide_subtract_fusion.1
  549.6 1.7 multiply_reduce_fusion
  551.9 3.2 divide_subtract_fusion
  (91 shorter events, 11.7 us)
Async XLA Ops:
  8.0 8.4 %copy-start.7 = (f32[256,400]{0,1:T(8,128)S(1)}, f32[256,400]{0,1:T(8,128)}, u32[]{:S(2)}) copy-start(f32[256,400]{0,1:T(8,128)} %param.12) | copy-start | bytes 1228804
  8.0 261.9 %all-reduce.6.cloned.1.call-start = ((), (), s32[]{:S(2)}) async-start(), calls=%async_computation.1 | async-start | bytes 6553600 | tf_op jit(solution)/shard_map/psum | solution.py:146
  9.7 20.0 %collective-permute-start = (bf16[1024,400]{0,1:T(8,128)(2,1)S(1)}, bf16[1024,400]{0,1:T(8,128)(2,1)S(1)}, u32[]{:S(2)}, u32[]{:S(2)}) collective-permute-start(bf16[1024,400]{0,1:T(8,128)(2,1)S(1)} %convert_element_type.98), channel_id=1, source_target_pairs={{256,0},{272,16},{288,32},{304,48},{320,64},{336,80},{352,96},{368... | collective-permute-start | bytes 2457608 | tf_op jit(solution)/shard_map/ppermute | solution.py:16
  31.0 1.9 copy-start.13
  37.3 0.6 copy-start.11
  42.6 2.6 copy-start.15
  42.6 3.2 copy-start.3
  46.7 11.0 %copy-start.1 = (f32[512,400]{0,1:T(8,128)S(1)}, f32[512,400]{0,1:T(8,128)}, u32[]{:S(2)}) copy-start(f32[512,400]{0,1:T(8,128)} %copy.46) | copy-start | bytes 2457604 | tf_op jit(solution)/shard_map/while
  46.7 11.0 %copy-start.2 = (f32[512,400]{0,1:T(8,128)S(1)}, f32[512,400]{0,1:T(8,128)}, u32[]{:S(2)}) copy-start(f32[512,400]{0,1:T(8,128)} %fusion.55) | copy-start | bytes 2457604 | tf_op jit(solution)/shard_map/while
  47.2 12.2 %copy-start = (f32[512,512]{0,1:T(8,128)}, f32[512,512]{0,1:T(8,128)S(1)}, u32[]{:S(2)}) copy-start(f32[512,512]{0,1:T(8,128)S(1)} %get-tuple-element.526) | copy-start | bytes 3145732 | tf_op jit(solution)/shard_map/while
  47.2 12.2 %copy-start.6 = (f32[512]{0:T(512)}, f32[512]{0:T(512)S(1)}, u32[]{:S(2)}) copy-start(f32[512]{0:T(512)S(1)} %get-tuple-element.522) | copy-start | bytes 6148 | tf_op jit(solution)/shard_map/while
  57.6 1.8 copy-start.9
  57.6 1.8 copy-start.10
  80.9 7.5 %copy-start.12 = (s32[512]{0:T(512)S(1)}, s32[512]{0:T(512)}, u32[]{:S(2)}) copy-start(s32[512]{0:T(512)} %copy-done.11) | copy-start | bytes 6148 | tf_op jit(solution)/shard_map/while
  88.4 4.5 copy-start.14
  97.2 0.6 copy-start.11
  102.5 2.6 copy-start.15
  102.5 3.2 copy-start.3
  106.6 7.8 %copy-start.1 = (f32[512,400]{0,1:T(8,128)S(1)}, f32[512,400]{0,1:T(8,128)}, u32[]{:S(2)}) copy-start(f32[512,400]{0,1:T(8,128)} %copy.46) | copy-start | bytes 2457604 | tf_op jit(solution)/shard_map/while
  106.6 7.8 %copy-start.2 = (f32[512,400]{0,1:T(8,128)S(1)}, f32[512,400]{0,1:T(8,128)}, u32[]{:S(2)}) copy-start(f32[512,400]{0,1:T(8,128)} %fusion.55) | copy-start | bytes 2457604 | tf_op jit(solution)/shard_map/while
  107.1 9.1 %copy-start = (f32[512,512]{0,1:T(8,128)}, f32[512,512]{0,1:T(8,128)S(1)}, u32[]{:S(2)}) copy-start(f32[512,512]{0,1:T(8,128)S(1)} %get-tuple-element.526) | copy-start | bytes 3145732 | tf_op jit(solution)/shard_map/while
  107.1 9.1 %copy-start.6 = (f32[512]{0:T(512)}, f32[512]{0:T(512)S(1)}, u32[]{:S(2)}) copy-start(f32[512]{0:T(512)S(1)} %get-tuple-element.522) | copy-start | bytes 6148 | tf_op jit(solution)/shard_map/while
  114.4 1.8 copy-start.9
  114.4 1.8 copy-start.10
  137.6 7.5 %copy-start.12 = (s32[512]{0:T(512)S(1)}, s32[512]{0:T(512)}, u32[]{:S(2)}) copy-start(s32[512]{0:T(512)} %copy-done.11) | copy-start | bytes 6148 | tf_op jit(solution)/shard_map/while
  145.1 4.5 copy-start.14
  154.1 393.5 %copy-start.17 = (f32[256]{0:T(256)S(1)}, f32[256]{0:T(256)}, u32[]{:S(2)}) copy-start(f32[256]{0:T(256)} %param.13) | copy-start | bytes 3076
  154.1 393.5 %copy-start.8 = (f32[256,400]{0,1:T(8,128)S(1)}, f32[256,400]{0,1:T(8,128)}, u32[]{:S(2)}) copy-start(f32[256,400]{0,1:T(8,128)} %param.12) | copy-start | bytes 1228804
  154.1 392.4 %all-reduce.4.cloned.1.call-start = ((), (), s32[]{:S(2)}) async-start(), calls=%async_computation | async-start | bytes 819200 | tf_op jit(solution)/shard_map/psum | solution.py:143
  269.9 279.7 %copy-start.5 = (f32[1024,400]{0,1:T(8,128)S(1)}, f32[1024,400]{0,1:T(8,128)}, u32[]{:S(2)}) copy-start(f32[1024,400]{0,1:T(8,128)} %get-tuple-element.398) | copy-start | bytes 4915204
  269.9 279.7 %collective-permute-start.1 = (f32[1024,400]{0,1:T(8,128)}, f32[1024,400]{0,1:T(8,128)}, u32[]{:S(2)}, u32[]{:S(2)}) collective-permute-start(f32[1024,400]{0,1:T(8,128)} %get-tuple-element.399), channel_id=1, source_target_pairs={{256,0},{272,16},{288,32},{304,48},{320,64},{336,80},{352,96},{368... | collective-permute-start | bytes 4915208 | tf_op jit(solution)/shard_map/ppermute | solution.py:16
  547.6 3.6 copy-start.16
  547.6 4.2 copy-start.4
Sparse Core Ops, SparseCore 0:
  154.3 115.5 all-reduce.5
Sparse Core Ops, SparseCore 1:
  275.7 270.8 all-reduce.3
where the time goes:
time: 564 us; the launch traced here: 562 us
  waiting for transfers between devices  400 us (71%)
  other arithmetic  62.3 us (11%)
  local copies, waits for them, and re-layouts  35.7 us (6%)
  matrix products  22.5 us (4%)
  blocking collectives  16 us (3%)
  between operations  15.6 us (3%)
  starting transfers between devices  10.3 us (2%)
    psum x1, waiting for transfers between devices, local(): rel_total = lax.psum(rel_grad, ('dom', 'bucket', 'depth'))  271 us
    psum x1, waiting for transfers between devices, local(): summed_own, summed_far = lax.psum((own_grad, far_grad), 'depth')  116 us
    scatter-add x4, other arithmetic, grad_part(): far_grad = far_grad.at[right_ids].add(half_coef[:, None] * queries.astype...  20.1 us
    all_gather x4, blocking collectives, merged(): pieces = jax.tree.map(lambda part: lax.all_gather(part, axis), value)  16 us
    scatter-add x2, other arithmetic, grad_part(): own_grad = own_grad.at[left_ids].add(query_grad * scaling)  14.3 us
    ppermute x2, waiting for transfers between devices, passed_along(): return lax.ppermute(block, axis, route)  13.1 us
    dot_general x6, matrix products, pick_rows(): jnp.dot(selector, table, preferred_element_type=jnp.float32)  12.7 us
  transfers between devices with their start and end apart: 4, of which 3 were waited for; matrix products, arithmetic and copies ran while one was open for 1% of the time, Pallas kernels for 0%

commit v1 on v0

v1 whole, which is shorter than its diff:
```python
import jax
import jax.numpy as jnp
from jax import lax
from jax.experimental import pallas as pl
from jax.experimental.pallas import tpu as pltpu
from jax.sharding import PartitionSpec as P

BLOCK = 512

entity_rate = 0.1
relation_rate = 1.0

F32 = jnp.float32
BF16 = jnp.bfloat16
NN = (((1,), (0,)), ((), ()))
NT = (((1,), (1,)), ((), ()))


def mm(a, b, dims=NN):
    return lax.dot_general(a, b, dims, preferred_element_type=F32)


def onehot(ids, rows):
    index = lax.broadcasted_iota(jnp.int32, (rows, ids.shape[1]), 0)
    return jnp.where(index == ids, 1.0, 0.0).astype(BF16)


def split(value, parts):
    out = []
    for _ in range(parts):
        piece = value.astype(BF16)
        out.append(piece)
        value = value - piece.astype(F32)
    return out


def prepare(own, rel, ends, rid, neg_a, neg_b, q, left, scale, count):
    rel_parts = split(rel[...], 3)
    ones = jnp.ones((neg_a.shape[1], 128), BF16)
    for c in range(q.shape[1] // BLOCK):
        lanes = slice(c * BLOCK, (c + 1) * BLOCK)
        picked = mm(own[...], onehot(ends[0:1, lanes], own.shape[1]))
        by_rel = onehot(rid[0:1, lanes], rel.shape[1])
        factor = sum(mm(part, by_rel) for part in rel_parts)
        q[:, lanes] = (picked * factor).astype(BF16)
        left[:, lanes] = picked.astype(BF16)
        scale[:, lanes] = factor
        hits = mm(onehot(neg_a[c : c + 1, :], own.shape[1]), ones)
        count[c] = hits + mm(onehot(neg_b[c : c + 1, :], own.shape[1]), ones)


CHUNK = 256


def block_lanes(block):
    return pl.ds(pl.multiple_of(block * BLOCK, BLOCK), BLOCK)


def softmax_coef(scores, times, right_ids, first, live):
    right = lax.broadcasted_iota(jnp.int32, scores.shape, 0) == right_ids
    positive = jnp.sum(jnp.where(right, scores, 0.0), axis=0, keepdims=True)
    masked = jnp.where(times > 0.0, scores, -3.0e38)
    peak = jnp.maximum(positive, jnp.max(masked, axis=0, keepdims=True))
    shifted = jnp.exp(masked - peak)
    top = jnp.exp(positive - peak)
    denom = top + jnp.sum(shifted * times, axis=0, keepdims=True)
    slot = lax.broadcasted_iota(jnp.int32, right_ids.shape, 1) + first
    active = jnp.where(slot < live, 1.0, 0.0)
    pos_coef = active * (top / denom - 1.0)
    weights = (shifted * (active / denom)).astype(BF16).astype(F32) * times
    return split(weights + jnp.where(right, pos_coef, 0.0), 2)


def own_block(
    block, live, ends, rid, far, q_hbm, left_hbm, scale_hbm, count_hbm,
    high_hbm, low_hbm, grad_hbm, rel_grad,
    q, left, scale, count, high, low, grad, sems,
):
    lanes = block_lanes(block[0])
    reads = [
        pltpu.make_async_copy(src, dst, sems.at[i])
        for i, (src, dst) in enumerate(
            [
                (q_hbm.at[:, lanes], q),
                (count_hbm.at[block[0]], count),
                (scale_hbm.at[:, lanes], scale),
                (left_hbm.at[:, lanes], left),
            ]
        )
    ]
    for read in reads:
        read.start()
    far_rows = far[...].T
    for read in reads[:2]:
        read.wait()
    times = jnp.tile(count[...], (1, CHUNK // 128))
    total, writes = None, []
    for c in range(BLOCK // CHUNK):
        part = slice(c * CHUNK, (c + 1) * CHUNK)
        first = pl.multiple_of(block[0] * BLOCK + c * CHUNK, CHUNK)
        ids = pl.ds(first, CHUNK)
        scores = mm(far_rows, q[:, part])
        upper, lower = softmax_coef(scores, times, ends[1:2, ids], first, live[0])
        high[:, part] = upper
        low[:, part] = lower
        query_grad = mm(far[...], upper) + mm(far[...], lower)
        if c == 0:
            for read in reads[2:]:
                read.wait()
        grad[:, part] = (query_grad * scale[:, part]).astype(BF16)
        for i, (src, dst) in enumerate([(high, high_hbm), (low, low_hbm), (grad, grad_hbm)]):
            write = pltpu.make_async_copy(
                src.at[:, part], dst.at[:, part], sems.at[4 + 3 * c + i]
            )
            write.start()
            writes.append(write)
        pieces = split(query_grad * left[:, part].astype(F32), 2)
        by_rel = onehot(rid[0:1, ids], rel_grad.shape[0])
        share = mm(by_rel, pieces[0], NT) + mm(by_rel, pieces[1], NT)
        total = share if total is None else total + share
    rel_grad[...] = total
    for write in writes:
        write.wait()


def dithered(value):
    row = lax.broadcasted_iota(jnp.int32, (value.shape[0], 1), 0).astype(F32) * 0.61803398875
    shift = (row - jnp.floor(row) - 0.5) * (1.0 / 256.0)
    return (value + value * shift).astype(BF16)


def other_block(
    block, live, ends, far_hbm, q_hbm, scale_hbm, count_hbm, high_hbm, low_hbm,
    far_grad, grad,
    far, q, scale, count, high, low, sems,
):
    lanes = block_lanes(1 - block[0])
    done = block_lanes(block[0])
    reads = [
        pltpu.make_async_copy(src, dst, sems.at[i])
        for i, (src, dst) in enumerate(
            [
                (far_hbm, far),
                (q_hbm, q),
                (count_hbm.at[1 - block[0]], count),
                (scale_hbm.at[:, lanes], scale),
                (high_hbm, high.at[:, done]),
                (low_hbm, low.at[:, done]),
            ]
        )
    ]
    for read in reads:
        read.start()
    for read in reads[:4]:
        read.wait()
    far_rows = far[...].T
    times = jnp.tile(count[...], (1, CHUNK // 128))
    for c in range(BLOCK // CHUNK):
        first = pl.multiple_of((1 - block[0]) * BLOCK + c * CHUNK, CHUNK)
        ids = pl.ds(first, CHUNK)
        scores = mm(far_rows, q[:, ids])
        upper, lower = softmax_coef(scores, times, ends[1:2, ids], first, live[0])
        high[:, ids] = upper
        low[:, ids] = lower
        query_grad = mm(far[...], upper) + mm(far[...], lower)
        part = slice(c * CHUNK, (c + 1) * CHUNK)
        grad[:, part] = (query_grad * scale[:, part]).astype(BF16)
    for read in reads[4:]:
        read.wait()
    for c in range(far_grad.shape[1] // CHUNK):
        part = slice(c * CHUNK, (c + 1) * CHUNK)
        both = mm(q[...], high[part, :], NT) + mm(q[...], low[part, :], NT)
        far_grad[:, part] = dithered(both)


def update_entities(
    block, ends, state, home, ent_hbm, grad_a, grad_b, new_state, new_hbm,
    ent, grad, new, sems,
):
    reads = [
        pltpu.make_async_copy(src, dst, sems.at[i])
        for i, (src, dst) in enumerate(
            [
                (grad_a, grad.at[:, block_lanes(block[0])]),
                (grad_b, grad.at[:, block_lanes(1 - block[0])]),
                (ent_hbm, ent),
            ]
        )
    ]
    for read in reads:
        read.start()
    for read in reads:
        read.wait()
    writes = []
    for c in range(ent.shape[1] // CHUNK):
        part = slice(c * CHUNK, (c + 1) * CHUNK)
        index = lax.broadcasted_iota(jnp.int32, (CHUNK, ends.shape[1]), 0) + c * CHUNK
        chosen = jnp.where(index == ends[0:1, :], 1.0, 0.0).astype(BF16)
        total = mm(grad[...], chosen, NT) + home[:, part].astype(F32)
        updated = state[0:1, part] + jnp.mean(total * total, axis=0, keepdims=True)
        new_state[0:1, part] = updated
        new[:, part] = ent[:, part] - entity_rate * total / jnp.sqrt(updated)
        write = pltpu.make_async_copy(new.at[:, part], new_hbm.at[:, part], sems.at[3 + c])
        write.start()
        writes.append(write)
    for write in writes:
        write.wait()


def sum_spread(pieces, out):
    out[...] = jnp.broadcast_to(jnp.sum(pieces[...], axis=0, keepdims=True), out.shape)


def update_relations(pieces, rel, state, out):
    total = jnp.sum(pieces[...], axis=0)
    updated = state[...] + jnp.mean(total * total, axis=1, keepdims=True)
    new = rel[...] - relation_rate * total / jnp.sqrt(updated)
    out[...] = jnp.broadcast_to(new[None], out.shape)


def call(kernel, args, outs, spaces, out_spaces, scratch=()):
    def spec(space, shape):
        if space == "b":
            return pl.BlockSpec(shape, lambda: (0,) * len(shape))
        return pl.BlockSpec(memory_space={"s": pltpu.SMEM, "v": pltpu.VMEM, "h": pltpu.HBM}[space])

    args = [
        pltpu.with_memory_space_constraint(arg, pltpu.HBM) if space in "hb" else arg
        for space, arg in zip(spaces, args, strict=True)
    ]
    return pl.pallas_call(
        kernel,
        out_shape=[
            pltpu.HBM(out.shape, out.dtype) if space in "hb" else out
            for space, out in zip(out_spaces, outs, strict=True)
        ],
        in_specs=[spec(space, arg.shape) for space, arg in zip(spaces, args, strict=True)],
        out_specs=[spec(space, out.shape) for space, out in zip(out_spaces, outs, strict=True)],
        scratch_shapes=list(scratch),
        compiler_params=pltpu.CompilerParams(vmem_limit_bytes=24 << 20),
    )(*args)


def passed_along(block, axis, distance):
    size = lax.axis_size(axis)
    return lax.ppermute(block, axis, [((i - distance) % size, i) for i in range(size)])


def mesh_groups():
    n_bucket, n_depth = lax.axis_size("bucket"), lax.axis_size("depth")
    n_x, n_y, n_core = 4, lax.axis_size("dom") // 8, 2

    def dom(x, y, core):
        return (x * n_y + y) * n_core + core

    along = [
        [dom(x, y, core) * n_bucket + z for y in range(n_y) for z in range(n_bucket)]
        for x in range(n_x)
        for core in range(n_core)
    ]
    across = [
        [
            dom(x, y, core) * n_depth + k
            for x in range(n_x)
            for core in range(n_core)
            for k in range(n_depth)
        ]
        for y in range(n_y)
    ]
    place = (lax.axis_index("dom") // n_core % n_y) * n_bucket + lax.axis_index("bucket")
    return along, across, place


def local(
    entities, entity_state, relations, relation_state, edge_ends, relation_ids, neg_ids, edge_count
):
    half_dom = lax.axis_size("dom") // 2
    rows, width = entities.shape
    n_rel = relations.shape[0]
    edges = relation_ids.shape[0]
    shape = jax.ShapeDtypeStruct
    rid = relation_ids.reshape(1, edges)

    neg_other = passed_along(neg_ids, "depth", 1)
    own = entities.T.astype(BF16)
    far = passed_along(own, "dom", half_dom)

    blocks = neg_ids.shape[0]
    wide, narrow = (width, edges), (width, BLOCK)
    q, left, scale, count = call(
        prepare,
        (own, relations.T, edge_ends, rid, neg_ids, neg_other),
        (shape(wide, BF16), shape(wide, BF16), shape(wide, F32), shape((blocks, rows, 128), F32)),
        "vvvvvv",
        "bbbb",
    )
    mine = lax.axis_index("depth").astype(jnp.int32).reshape(1)
    mat = (rows, BLOCK)
    high, low, grad_a, rel_grad = call(
        own_block,
        (mine, edge_count, edge_ends, rid, far, q, left, scale, count),
        (shape(mat, BF16), shape(mat, BF16), shape(narrow, BF16), shape((n_rel, width), F32)),
        "ssvvvhhhh",
        "hhhb",
        (
            pltpu.VMEM(narrow, BF16),
            pltpu.VMEM(narrow, BF16),
            pltpu.VMEM(narrow, F32),
            pltpu.VMEM((rows, 128), F32),
            pltpu.VMEM(mat, BF16),
            pltpu.VMEM(mat, BF16),
            pltpu.VMEM(narrow, BF16),
            pltpu.SemaphoreType.DMA((10,)),
        ),
    )
    along, across, place = mesh_groups()
    groups = len(along[0])
    share = n_rel // groups

    def exchange(pieces, axis, index_groups):
        return lax.all_to_all(pieces, axis, 0, 0, axis_index_groups=index_groups)

    pieces = exchange(rel_grad.reshape(groups, share, width), ("dom", "bucket"), along)

    far_grad, grad_b = call(
        other_block,
        (mine, edge_count, edge_ends, far, q, scale, count, high, low),
        (shape((width, rows), BF16), shape(narrow, BF16)),
        "ssvhhhhhh",
        "vb",
        (
            pltpu.VMEM((width, rows), BF16),
            pltpu.VMEM(wide, BF16),
            pltpu.VMEM(narrow, F32),
            pltpu.VMEM((rows, 128), F32),
            pltpu.VMEM((rows, edges), BF16),
            pltpu.VMEM((rows, edges), BF16),
            pltpu.SemaphoreType.DMA((6,)),
        ),
    )
    home_grad = passed_along(far_grad, "dom", half_dom)

    first = place * share
    my_rel = lax.dynamic_slice_in_dim(relations, first, share, 0)
    my_state = lax.dynamic_slice_in_dim(relation_state, first, share, 0)[:, None]
    pieces, far_grad = lax.optimization_barrier((pieces, far_grad))
    stack = (shape((len(across[0]), share, width), F32),)
    (partial,) = call(sum_spread, (pieces,), stack, "v", "b")
    totals = exchange(partial, ("dom", "depth"), across)
    stack = (shape((groups, share, width), F32),)
    (new_rel,) = call(update_relations, (totals, my_rel, my_state), stack, "vvv", "b")
    new_relations = exchange(new_rel, ("dom", "bucket"), along).reshape(n_rel, width)

    new_state, new_entities = call(
        update_entities,
        (mine, edge_ends, entity_state.reshape(1, rows), home_grad, entities.T, grad_a, grad_b),
        (shape((1, rows), F32), shape((width, rows), F32)),
        "svvvhhh",
        "vh",
        (
            pltpu.VMEM((width, rows), F32),
            pltpu.VMEM(wide, BF16),
            pltpu.VMEM((width, rows), F32),
            pltpu.SemaphoreType.DMA((7,)),
        ),
    )
    return (new_entities.T, new_state.reshape(rows), new_relations)


def solution(mesh):
    return jax.shard_map(
        local,
        mesh=mesh,
        in_specs=(
            P(("dom", "bucket"), None),
            P(("dom", "bucket")),
            P(),
            P(),
            P(None, ("dom", "bucket")),
            P(("dom", "bucket")),
            P(("dom", "bucket"), "depth"),
            P(("dom", "bucket")),
        ),
        out_specs=(P(("dom", "bucket"), None), P(("dom", "bucket")), P()),
        check_vma=False,
    )
```

time: 564 us -> 110 us (0.20)
  the two profiles are of different devices: /device:TPU:1 before, /device:TPU:8 now
where the time goes in v1:
time: 110 us; the launch traced here: 109 us
  starting transfers between devices  43.8 us (40%)
  waiting for transfers between devices  33.7 us (31%)
  Pallas kernels  27.3 us (25%)
  other arithmetic  1.6 us (1%)
  between operations  1.44 us (1%)
  local copies, waits for them, and re-layouts  1.32 us (1%)
    all_to_all x3, starting transfers between devices, exchange(): return lax.all_to_all(pieces, axis, 0, 0, axis_index_groups=index_groups)  29.3 us
    pallas_call x6, Pallas kernels, call(): pl.pallas_call(kernel, out_shape=[pltpu.HBM(out.shape, out.dtype) if spac...  27.3 us
    ppermute x3, waiting for transfers between devices, passed_along(): lax.ppermute(block, axis, [((i - distance) % size, i) for i in range(size)])  18.9 us
    all_to_all x3, waiting for transfers between devices, exchange(): return lax.all_to_all(pieces, axis, 0, 0, axis_index_groups=index_groups)  14.8 us
    ppermute x3, starting transfers between devices, passed_along(): lax.ppermute(block, axis, [((i - distance) % size, i) for i in range(size)])  14.5 us
  transfers between devices with their start and end apart: 6, of which 6 were waited for; matrix products, arithmetic and copies ran while one was open for 0% of the time, Pallas kernels for 17%

profile of v1, /device:TPU:8, one launch (start us, length us, event | category | flops | bytes accessed | tf_op | source)
XLA Modules:
  0.0 109.1 jit_solution(8530936455080753698)
XLA Ops:
  0.6 0.0 copy-start
  0.6 0.0 copy-start.5
  0.7 0.0 copy-start.4
  0.7 0.0 copy-start.2
  0.7 0.0 copy-start.3
  0.7 1.6 %bitcast_convert_fusion.own = bf16[400,1024]{1,0:T(8,128)(2,1)S(1)} fusion(f32[1024,400]{0,1:T(8,128)} %param.8), kind=kLoop, calls=%fused_computation.2 | loop fusion | flops 409600 | bytes 2457600 | tf_op jit(solution)/shard_map/convert_element_type | solution.py:285
  2.3 4.9 %collective-permute-start = (bf16[400,1024]{1,0:T(8,128)(2,1)S(1)}, bf16[400,1024]{1,0:T(8,128)(2,1)S(1)}, u32[]{:S(2)}, u32[]{:S(2)}) collective-permute-start(bf16[400,1024]{1,0:T(8,128)(2,1)S(1)} %bitcast_convert_fusion.own), channel_id=1, source_target_pairs={{256,0},{272,16},{288,32},{304,48},{320,64},{336,80},{352,96},{368... | collective-permute-start | bytes 2457608 | tf_op jit(solution)/shard_map/ppermute | solution.py:246
  7.2 0.0 copy-done.5
  7.2 4.7 %collective-permute-start.1 = (s32[2,512]{1,0:T(2,128)S(1)}, s32[2,512]{1,0:T(2,128)S(1)}, u32[]{:S(2)}, u32[]{:S(2)}) collective-permute-start(s32[2,512]{1,0:T(2,128)S(1)} %copy-done.5), channel_id=1, source_target_pairs={{1,0},{0,1},{3,2},{2,3},{5,4},{4,5},{7,6},{6,7},{9,8},{8,9},{11,10... | collective-permute-start | bytes 12296 | tf_op jit(solution)/shard_map/ppermute | solution.py:246
  12.6 0.9 collective-permute-done.1.neg_b
  13.5 0.0 copy-done.4
  13.5 0.0 copy-done.2
  13.5 0.0 copy-done.3
  13.5 4.7 %shard_map.103 = (bf16[400,1024]{1,0:T(8,128)(2,1)}, bf16[400,1024]{1,0:T(8,128)(2,1)}, f32[400,1024]{1,0:T(8,128)}, f32[2,1024,128]{2,1,0:T(8,128)}) custom-call(bf16[400,1024]{1,0:T(8,128)(2,1)S(1)} %bitcast_convert_fusion.own, f32[400,256]{1,0:T(8,128)S(1)} %bitcast.12, s32[2,1024]{1,0:T(2,128)S(1)} %copy-done.3, s32[1,1024]{1,0:T(1,128)S(1)} %bitcast.13, ...), custom_call_target="tpu_custom_call" | custom-call | tf_op jit(solution)/shard_map/pallas_call | solution.py:231
  18.2 7.5 %collective-permute-done.far.far_hbm = bf16[400,1024]{1,0:T(8,128)(2,1)S(1)} collective-permute-done((bf16[400,1024]{1,0:T(8,128)(2,1)S(1)}, bf16[400,1024]{1,0:T(8,128)(2,1)S(1)}, u32[]{:S(2)}, u32[]{:S(2)}) %collective-permute-start) | collective-permute-done | bytes 819232 | tf_op jit(solution)/shard_map/ppermute | solution.py:246
  25.7 0.0 copy-start.1
  25.7 8.3 %shard_map.104 = (bf16[1024,512]{1,0:T(8,128)(2,1)}, bf16[1024,512]{1,0:T(8,128)(2,1)}, bf16[400,512]{1,0:T(8,128)(2,1)}, f32[256,400]{1,0:T(8,128)}) custom-call(s32[1]{0:T(128)} %bitcast.block, s32[1]{0:T(128)S(6)} %copy.15.live, s32[2,1024]{1,0:T(2,128)S(1)} %copy-done.3, s32[1,1024]{1,0:T(1,128)S(1)} %bitcast.14, ...), custom_call_target="tpu_custom_call" | custom-call | tf_op jit(solution)/shard_map/pallas_call | solution.py:231
  34.0 0.0 copy-done.1
  34.0 15.3 %all-to-all-start = ((f32[32,8,400]{2,1,0:T(8,128)}), f32[32,8,400]{2,1,0:T(8,128)S(1)}, u32[]{:S(2)}, u32[]{:S(2)}) async-start(f32[32,8,400]{2,1,0:T(8,128)} %bitcast.18), calls=%async_computation | async-start | bytes 1048576 | tf_op jit(solution)/shard_map/all_to_all | solution.py:321
  49.3 7.9 %shard_map.105 = (bf16[400,1024]{1,0:T(8,128)(2,1)S(1)}, bf16[400,512]{1,0:T(8,128)(2,1)}) custom-call(s32[1]{0:T(128)} %bitcast.block, s32[1]{0:T(128)S(6)} %copy.15.live, s32[2,1024]{1,0:T(2,128)S(1)} %copy-done.3, bf16[400,1024]{1,0:T(8,128)(2,1)} %copy-done.1, bf16[400,1024]{1,0:T(8,128)(2,1)} %get-tuple-element.16.q_hbm, ...), custom_call_target="tpu_custom_call" | custom-call | tf_op jit(solution)/shard_map/pallas_call | solution.py:231
  57.2 8.4 %all-to-all-done.pieces = f32[32,8,400]{2,1,0:T(8,128)S(1)} async-done(((f32[32,8,400]{2,1,0:T(8,128)}), f32[32,8,400]{2,1,0:T(8,128)S(1)}, u32[]{:S(2)}, u32[]{:S(2)}) %all-to-all-start) | async-done | bytes 409632 | tf_op jit(solution)/shard_map/all_to_all | solution.py:321
  65.6 0.8 shard_map.107
  66.4 0.0 copy-start.6
  66.4 7.9 %all-to-all-start.1 = ((f32[16,8,400]{2,1,0:T(8,128)}), f32[16,8,400]{2,1,0:T(8,128)S(1)}, u32[]{:S(2)}, u32[]{:S(2)}) async-start(f32[16,8,400]{2,1,0:T(8,128)} %shard_map.107), calls=%async_computation.1 | async-start | bytes 524288 | tf_op jit(solution)/shard_map/all_to_all | solution.py:321
  74.3 0.1 constant_dynamic-slice_fusion
  74.4 4.9 %collective-permute-start.2 = (bf16[400,1024]{1,0:T(8,128)(2,1)S(1)}, bf16[400,1024]{1,0:T(8,128)(2,1)S(1)}, u32[]{:S(2)}, u32[]{:S(2)}) collective-permute-start(bf16[400,1024]{1,0:T(8,128)(2,1)S(1)} %get-tuple-element.22), channel_id=1, source_target_pairs={{256,0},{272,16},{288,32},{304,48},{320,64},{336,80},{352,96},{368... | collective-permute-start | bytes 2457608 | tf_op jit(solution)/shard_map/ppermute | solution.py:246
  79.3 0.0 copy-done
  79.3 0.1 dynamic-slice_bitcast_fusion
  79.4 0.1 copy.14.rel
  79.5 0.1 copy.12.state
  79.6 1.6 %all-to-all-done.1.pieces = f32[16,8,400]{2,1,0:T(8,128)S(1)} async-done(((f32[16,8,400]{2,1,0:T(8,128)}), f32[16,8,400]{2,1,0:T(8,128)S(1)}, u32[]{:S(2)}, u32[]{:S(2)}) %all-to-all-start.1) | async-done | bytes 204832 | tf_op jit(solution)/shard_map/all_to_all | solution.py:321
  81.2 1.0 shard_map.108
  82.2 6.1 %all-to-all-start.2 = ((f32[32,8,400]{2,1,0:T(8,128)}), f32[32,8,400]{2,1,0:T(8,128)S(1)}, u32[]{:S(2)}, u32[]{:S(2)}) async-start(f32[32,8,400]{2,1,0:T(8,128)} %shard_map.108), calls=%async_computation.2 | async-start | bytes 1048576 | tf_op jit(solution)/shard_map/all_to_all | solution.py:321
  88.3 10.5 %collective-permute-done.2.home = bf16[400,1024]{1,0:T(8,128)(2,1)S(1)} collective-permute-done((bf16[400,1024]{1,0:T(8,128)(2,1)S(1)}, bf16[400,1024]{1,0:T(8,128)(2,1)S(1)}, u32[]{:S(2)}, u32[]{:S(2)}) %collective-permute-start.2) | collective-permute-done | bytes 819232 | tf_op jit(solution)/shard_map/ppermute | solution.py:246
  98.8 0.0 copy-done.6
  98.8 4.6 %shard_map.106 = (f32[1,1024]{1,0:T(1,128)}, f32[400,1024]{1,0:T(8,128)}) custom-call(s32[1]{0:T(128)} %bitcast.block, s32[2,1024]{1,0:T(2,128)S(1)} %copy-done.3, f32[1,1024]{1,0:T(1,128)S(1)} %bitcast.15, bf16[400,1024]{1,0:T(8,128)(2,1)S(1)} %collective-permute-done.2.home, f32[400,1024]{1,0:T(8,128)} %bitcast.16, ...), custom_call_target="tpu_custom_call" | custom-call | tf_op jit(solution)/shard_map/pallas_call | solution.py:231
  103.4 4.8 %all-to-all-done.2 = f32[32,8,400]{2,1,0:T(8,128)S(1)} async-done(((f32[32,8,400]{2,1,0:T(8,128)}), f32[32,8,400]{2,1,0:T(8,128)S(1)}, u32[]{:S(2)}, u32[]{:S(2)}) %all-to-all-start.2) | async-done | bytes 409632 | tf_op jit(solution)/shard_map/all_to_all | solution.py:321
  108.2 0.9 copy.13
Async XLA Ops:
  0.6 78.7 %copy-start = (f32[256]{0:T(256)S(1)}, f32[256]{0:T(256)}, u32[]{:S(2)}) copy-start(f32[256]{0:T(256)} %param.11) | copy-start | bytes 3076
  0.6 6.6 %copy-start.5 = (s32[2,512]{1,0:T(2,128)S(1)}, s32[2,512]{1,0:T(2,128)}, u32[]{:S(2)}) copy-start(s32[2,512]{1,0:T(2,128)} %neg_a.1) | copy-start | bytes 12292
  0.7 12.9 %copy-start.4 = (s32[1024]{0:T(1024)S(1)}, s32[1024]{0:T(1024)}, u32[]{:S(2)}) copy-start(s32[1024]{0:T(1024)} %param.13) | copy-start | bytes 12292
  0.7 12.9 %copy-start.2 = (f32[256,400]{0,1:T(8,128)S(1)}, f32[256,400]{0,1:T(8,128)}, u32[]{:S(2)}) copy-start(f32[256,400]{0,1:T(8,128)} %param.10) | copy-start | bytes 1228804
  0.7 12.8 %copy-start.3 = (s32[2,1024]{1,0:T(2,128)S(1)}, s32[2,1024]{1,0:T(2,128)}, u32[]{:S(2)}) copy-start(s32[2,1024]{1,0:T(2,128)} %ends.7) | copy-start | bytes 24580
  2.3 23.4 %collective-permute-start = (bf16[400,1024]{1,0:T(8,128)(2,1)S(1)}, bf16[400,1024]{1,0:T(8,128)(2,1)S(1)}, u32[]{:S(2)}, u32[]{:S(2)}) collective-permute-start(bf16[400,1024]{1,0:T(8,128)(2,1)S(1)} %bitcast_convert_fusion.own), channel_id=1, source_target_pairs={{256,0},{272,16},{288,32},{304,48},{320,64},{336,80},{352,96},{368... | collective-permute-start | bytes 2457608 | tf_op jit(solution)/shard_map/ppermute | solution.py:246
  7.2 6.3 %collective-permute-start.1 = (s32[2,512]{1,0:T(2,128)S(1)}, s32[2,512]{1,0:T(2,128)S(1)}, u32[]{:S(2)}, u32[]{:S(2)}) collective-permute-start(s32[2,512]{1,0:T(2,128)S(1)} %copy-done.5), channel_id=1, source_target_pairs={{1,0},{0,1},{3,2},{2,3},{5,4},{4,5},{7,6},{6,7},{9,8},{8,9},{11,10... | collective-permute-start | bytes 12296 | tf_op jit(solution)/shard_map/ppermute | solution.py:246
  25.7 8.4 %copy-start.1 = (bf16[400,1024]{1,0:T(8,128)(2,1)}, bf16[400,1024]{1,0:T(8,128)(2,1)S(1)}, u32[]{:S(2)}) copy-start(bf16[400,1024]{1,0:T(8,128)(2,1)S(1)} %collective-permute-done.far.far_hbm) | copy-start | bytes 2457604
  34.0 31.6 %all-to-all-start = ((f32[32,8,400]{2,1,0:T(8,128)}), f32[32,8,400]{2,1,0:T(8,128)S(1)}, u32[]{:S(2)}, u32[]{:S(2)}) async-start(f32[32,8,400]{2,1,0:T(8,128)} %bitcast.18), calls=%async_computation | async-start | bytes 1048576 | tf_op jit(solution)/shard_map/all_to_all | solution.py:321
  66.4 32.4 %copy-start.6 = (f32[1024]{0:T(1024)S(1)}, f32[1024]{0:T(1024)}, u32[]{:S(2)}) copy-start(f32[1024]{0:T(1024)} %param.9) | copy-start | bytes 12292
  66.4 14.8 %all-to-all-start.1 = ((f32[16,8,400]{2,1,0:T(8,128)}), f32[16,8,400]{2,1,0:T(8,128)S(1)}, u32[]{:S(2)}, u32[]{:S(2)}) async-start(f32[16,8,400]{2,1,0:T(8,128)} %shard_map.107), calls=%async_computation.1 | async-start | bytes 524288 | tf_op jit(solution)/shard_map/all_to_all | solution.py:321
  74.4 24.4 %collective-permute-start.2 = (bf16[400,1024]{1,0:T(8,128)(2,1)S(1)}, bf16[400,1024]{1,0:T(8,128)(2,1)S(1)}, u32[]{:S(2)}, u32[]{:S(2)}) collective-permute-start(bf16[400,1024]{1,0:T(8,128)(2,1)S(1)} %get-tuple-element.22), channel_id=1, source_target_pairs={{256,0},{272,16},{288,32},{304,48},{320,64},{336,80},{352,96},{368... | collective-permute-start | bytes 2457608 | tf_op jit(solution)/shard_map/ppermute | solution.py:246
  82.2 26.0 %all-to-all-start.2 = ((f32[32,8,400]{2,1,0:T(8,128)}), f32[32,8,400]{2,1,0:T(8,128)S(1)}, u32[]{:S(2)}, u32[]{:S(2)}) async-start(f32[32,8,400]{2,1,0:T(8,128)} %shard_map.108), calls=%async_computation.2 | async-start | bytes 1048576 | tf_op jit(solution)/shard_map/all_to_all | solution.py:321

commit v2 on v1

--- a/solution.py
+++ b/solution.py
@@ -49,7 +49,8 @@
         count[c] = hits + mm(onehot(neg_b[c : c + 1, :], own.shape[1]), ones)
 
 
-CHUNK = 256
+CHUNK = 512
+TILE = 256
 
 
 def block_lanes(block):
@@ -72,53 +73,37 @@
 
 
 def own_block(
-    block, live, ends, rid, far, q_hbm, left_hbm, scale_hbm, count_hbm,
-    high_hbm, low_hbm, grad_hbm, rel_grad,
-    q, left, scale, count, high, low, grad, sems,
+    block, live, ends, rid, far, q, left, scale, count,
+    high_hbm, low_hbm, grad_hbm, rel_hbm,
+    high, low, grad, rel_grad, sems,
 ):
-    lanes = block_lanes(block[0])
-    reads = [
-        pltpu.make_async_copy(src, dst, sems.at[i])
-        for i, (src, dst) in enumerate(
-            [
-                (q_hbm.at[:, lanes], q),
-                (count_hbm.at[block[0]], count),
-                (scale_hbm.at[:, lanes], scale),
-                (left_hbm.at[:, lanes], left),
-            ]
-        )
-    ]
-    for read in reads:
-        read.start()
     far_rows = far[...].T
-    for read in reads[:2]:
-        read.wait()
-    times = jnp.tile(count[...], (1, CHUNK // 128))
+    times = jnp.tile(count[block[0]], (1, CHUNK // 128))
     total, writes = None, []
     for c in range(BLOCK // CHUNK):
         part = slice(c * CHUNK, (c + 1) * CHUNK)
         first = pl.multiple_of(block[0] * BLOCK + c * CHUNK, CHUNK)
         ids = pl.ds(first, CHUNK)
-        scores = mm(far_rows, q[:, part])
+        scores = mm(far_rows, q[:, ids])
         upper, lower = softmax_coef(scores, times, ends[1:2, ids], first, live[0])
         high[:, part] = upper
         low[:, part] = lower
         query_grad = mm(far[...], upper) + mm(far[...], lower)
-        if c == 0:
-            for read in reads[2:]:
-                read.wait()
-        grad[:, part] = (query_grad * scale[:, part]).astype(BF16)
+        grad[:, part] = (query_grad * scale[:, ids]).astype(BF16)
         for i, (src, dst) in enumerate([(high, high_hbm), (low, low_hbm), (grad, grad_hbm)]):
             write = pltpu.make_async_copy(
-                src.at[:, part], dst.at[:, part], sems.at[4 + 3 * c + i]
+                src.at[:, part], dst.at[:, part], sems.at[3 * c + i]
             )
             write.start()
             writes.append(write)
-        pieces = split(query_grad * left[:, part].astype(F32), 2)
+        pieces = split(query_grad * left[:, ids].astype(F32), 2)
         by_rel = onehot(rid[0:1, ids], rel_grad.shape[0])
         share = mm(by_rel, pieces[0], NT) + mm(by_rel, pieces[1], NT)
         total = share if total is None else total + share
     rel_grad[...] = total
+    write = pltpu.make_async_copy(rel_grad, rel_hbm, sems.at[3 * (BLOCK // CHUNK)])
+    write.start()
+    writes.append(write)
     for write in writes:
         write.wait()
 
@@ -167,8 +152,8 @@
         grad[:, part] = (query_grad * scale[:, part]).astype(BF16)
     for read in reads[4:]:
         read.wait()
-    for c in range(far_grad.shape[1] // CHUNK):
-        part = slice(c * CHUNK, (c + 1) * CHUNK)
+    for c in range(far_grad.shape[1] // TILE):
+        part = slice(c * TILE, (c + 1) * TILE)
         both = mm(q[...], high[part, :], NT) + mm(q[...], low[part, :], NT)
         far_grad[:, part] = dithered(both)
 
@@ -192,9 +177,9 @@
     for read in reads:
         read.wait()
     writes = []
-    for c in range(ent.shape[1] // CHUNK):
-        part = slice(c * CHUNK, (c + 1) * CHUNK)
-        index = lax.broadcasted_iota(jnp.int32, (CHUNK, ends.shape[1]), 0) + c * CHUNK
+    for c in range(ent.shape[1] // TILE):
+        part = slice(c * TILE, (c + 1) * TILE)
+        index = lax.broadcasted_iota(jnp.int32, (TILE, ends.shape[1]), 0) + c * TILE
         chosen = jnp.where(index == ends[0:1, :], 1.0, 0.0).astype(BF16)
         total = mm(grad[...], chosen, NT) + home[:, part].astype(F32)
         updated = state[0:1, part] + jnp.mean(total * total, axis=0, keepdims=True)
@@ -292,7 +277,7 @@
         (own, relations.T, edge_ends, rid, neg_ids, neg_other),
         (shape(wide, BF16), shape(wide, BF16), shape(wide, F32), shape((blocks, rows, 128), F32)),
         "vvvvvv",
-        "bbbb",
+        "vvvv",
     )
     mine = lax.axis_index("depth").astype(jnp.int32).reshape(1)
     mat = (rows, BLOCK)
@@ -300,17 +285,14 @@
         own_block,
         (mine, edge_count, edge_ends, rid, far, q, left, scale, count),
         (shape(mat, BF16), shape(mat, BF16), shape(narrow, BF16), shape((n_rel, width), F32)),
-        "ssvvvhhhh",
-        "hhhb",
+        "ssvvvvvvv",
+        "hhhh",
         (
-            pltpu.VMEM(narrow, BF16),
-            pltpu.VMEM(narrow, BF16),
-            pltpu.VMEM(narrow, F32),
-            pltpu.VMEM((rows, 128), F32),
             pltpu.VMEM(mat, BF16),
             pltpu.VMEM(mat, BF16),
             pltpu.VMEM(narrow, BF16),
-            pltpu.SemaphoreType.DMA((10,)),
+            pltpu.VMEM((n_rel, width), F32),
+            pltpu.SemaphoreType.DMA((3 * (BLOCK // CHUNK) + 1,)),
         ),
     )
     along, across, place = mesh_groups()

time: 110 us -> 107 us (0.973)
  Pallas kernels: 27.3 us -> 21.9 us
    pallas_call x6, Pallas kernels: 27.3 us -> 21.9 us  [call(): pl.pallas_call(kernel, out_shape=[pltpu.HBM(out.shape, out.dtype) if spac...]
  transfers between devices with their start and end apart: 6 -> 6, of which waited for: 6 -> 6; matrix products, arithmetic and copies ran while one was open for 0% -> 0% of each run, Pallas kernels for 17% -> 16%
where the time goes in v2:
time: 107 us; the launch traced here: 106 us
  starting transfers between devices  43.6 us (41%)
  waiting for transfers between devices  34.5 us (32%)
  Pallas kernels  21.9 us (20%)
  other arithmetic  2.49 us (2%)
  local copies, waits for them, and re-layouts  2.35 us (2%)
  between operations  1.48 us (1%)
    all_to_all x3, starting transfers between devices, exchange(): return lax.all_to_all(pieces, axis, 0, 0, axis_index_groups=index_groups)  29.1 us
    pallas_call x6, Pallas kernels, call(): pl.pallas_call(kernel, out_shape=[pltpu.HBM(out.shape, out.dtype) if spac...  21.9 us
    ppermute x3, waiting for transfers between devices, passed_along(): lax.ppermute(block, axis, [((i - distance) % size, i) for i in range(size)])  18.8 us
    all_to_all x3, waiting for transfers between devices, exchange(): return lax.all_to_all(pieces, axis, 0, 0, axis_index_groups=index_groups)  15.7 us
    ppermute x3, starting transfers between devices, passed_along(): lax.ppermute(block, axis, [((i - distance) % size, i) for i in range(size)])  14.5 us
    convert_element_type x1, other arithmetic, local(): own = entities.T.astype(BF16)  2.49 us
  transfers between devices with their start and end apart: 6, of which 6 were waited for; matrix products, arithmetic and copies ran while one was open for 0% of the time, Pallas kernels for 16%

profile of v2, /device:TPU:8, one launch (start us, length us, event | category | flops | bytes accessed | tf_op | source)
XLA Modules:
  0.0 106.2 jit_solution(17063506047670895272)
XLA Ops:
  0.6 0.0 copy-start
  0.6 0.0 copy-start.9
  0.7 0.0 copy-start.8
  0.7 0.0 copy-start.7
  0.7 2.5 %bitcast_convert_fusion.own = bf16[400,1024]{1,0:T(8,128)(2,1)} fusion(f32[1024,400]{0,1:T(8,128)} %param.8), kind=kLoop, calls=%fused_computation.2 | loop fusion | flops 409600 | bytes 2457600 | tf_op jit(solution)/shard_map/convert_element_type | solution.py:270
  3.2 4.9 %collective-permute-start = (bf16[400,1024]{1,0:T(8,128)(2,1)}, bf16[400,1024]{1,0:T(8,128)(2,1)S(1)}, u32[]{:S(2)}, u32[]{:S(2)}) collective-permute-start(bf16[400,1024]{1,0:T(8,128)(2,1)} %bitcast_convert_fusion.own), channel_id=1, source_target_pairs={{256,0},{272,16},{288,32},{304,48},{320,64},{336,80},{352,96},{368... | collective-permute-start | bytes 2457608 | tf_op jit(solution)/shard_map/ppermute | solution.py:231
  8.1 0.0 copy-done.9
  8.1 4.7 %collective-permute-start.1 = (s32[2,512]{1,0:T(2,128)S(1)}, s32[2,512]{1,0:T(2,128)S(1)}, u32[]{:S(2)}, u32[]{:S(2)}) collective-permute-start(s32[2,512]{1,0:T(2,128)S(1)} %copy-done.9), channel_id=1, source_target_pairs={{1,0},{0,1},{3,2},{2,3},{5,4},{4,5},{7,6},{6,7},{9,8},{8,9},{11,10... | collective-permute-start | bytes 12296 | tf_op jit(solution)/shard_map/ppermute | solution.py:231
  13.5 0.9 collective-permute-done.1.neg_b
  14.4 0.0 copy-done.8
  14.4 0.0 copy-done.7
  14.4 0.0 copy-start.5
  14.4 1.0 copy-done.5
  15.4 3.9 %shard_map.103 = (bf16[400,1024]{1,0:T(8,128)(2,1)S(1)}, bf16[400,1024]{1,0:T(8,128)(2,1)S(1)}, f32[400,1024]{1,0:T(8,128)S(1)}, f32[2,1024,128]{2,1,0:T(8,128)S(1)}) custom-call(bf16[400,1024]{1,0:T(8,128)(2,1)} %bitcast_convert_fusion.own, f32[400,256]{1,0:T(8,128)S(1)} %bitcast.12, s32[2,1024]{1,0:T(2,128)S(1)} %copy-done.7, s32[1,1024]{1,0:T(1,128)S(1)} %bitcast.13, ...), custom_call_target="tpu_custom_call" | custom-call | tf_op jit(solution)/shard_map/pallas_call | solution.py:216
  19.3 0.0 copy-start.1
  19.3 0.0 copy-start.2
  19.3 0.0 copy-start.4
  19.3 7.4 %collective-permute-done.far.far_hbm = bf16[400,1024]{1,0:T(8,128)(2,1)S(1)} collective-permute-done((bf16[400,1024]{1,0:T(8,128)(2,1)}, bf16[400,1024]{1,0:T(8,128)(2,1)S(1)}, u32[]{:S(2)}, u32[]{:S(2)}) %collective-permute-start) | collective-permute-done | bytes 819232 | tf_op jit(solution)/shard_map/ppermute | solution.py:231
  26.7 0.0 copy-start.3
  26.7 4.5 %shard_map.104 = (bf16[1024,512]{1,0:T(8,128)(2,1)}, bf16[1024,512]{1,0:T(8,128)(2,1)}, bf16[400,512]{1,0:T(8,128)(2,1)}, f32[256,400]{1,0:T(8,128)}) custom-call(s32[1]{0:T(128)} %bitcast.block, s32[1]{0:T(128)S(6)} %copy.15.live, s32[2,1024]{1,0:T(2,128)S(1)} %copy-done.7, s32[1,1024]{1,0:T(1,128)S(1)} %bitcast.14, ...), custom_call_target="tpu_custom_call" | custom-call | tf_op jit(solution)/shard_map/pallas_call | solution.py:216
  31.2 0.0 copy-done.1
  31.2 0.0 copy-done.2
  31.2 0.0 copy-done.4
  31.2 0.0 copy-done.3
  31.2 15.1 %all-to-all-start = ((f32[32,8,400]{2,1,0:T(8,128)}), f32[32,8,400]{2,1,0:T(8,128)S(1)}, u32[]{:S(2)}, u32[]{:S(2)}) async-start(f32[32,8,400]{2,1,0:T(8,128)} %bitcast.18), calls=%async_computation | async-start | bytes 1048576 | tf_op jit(solution)/shard_map/all_to_all | solution.py:303
  46.3 0.0 copy-start.6
  46.3 7.1 %shard_map.105 = (bf16[400,1024]{1,0:T(8,128)(2,1)S(1)}, bf16[400,512]{1,0:T(8,128)(2,1)}) custom-call(s32[1]{0:T(128)} %bitcast.block, s32[1]{0:T(128)S(6)} %copy.15.live, s32[2,1024]{1,0:T(2,128)S(1)} %copy-done.7, bf16[400,1024]{1,0:T(8,128)(2,1)} %copy-done.3, bf16[400,1024]{1,0:T(8,128)(2,1)} %copy-done.4, f32[400,1024]{1,0:T(8,128)} %copy-done.1, ...), custom_call_target="tpu_custom_call" | custom-call | tf_op jit(solution)/shard_map/pallas_call | solution.py:216
  53.5 9.3 %all-to-all-done.pieces = f32[32,8,400]{2,1,0:T(8,128)S(1)} async-done(((f32[32,8,400]{2,1,0:T(8,128)}), f32[32,8,400]{2,1,0:T(8,128)S(1)}, u32[]{:S(2)}, u32[]{:S(2)}) %all-to-all-start) | async-done | bytes 409632 | tf_op jit(solution)/shard_map/all_to_all | solution.py:303
  62.8 0.8 shard_map.107
  63.6 0.0 copy-start.10
  63.6 7.9 %all-to-all-start.1 = ((f32[16,8,400]{2,1,0:T(8,128)}), f32[16,8,400]{2,1,0:T(8,128)S(1)}, u32[]{:S(2)}, u32[]{:S(2)}) async-start(f32[16,8,400]{2,1,0:T(8,128)} %shard_map.107), calls=%async_computation.1 | async-start | bytes 524288 | tf_op jit(solution)/shard_map/all_to_all | solution.py:303
  71.4 0.0 copy-done.6
  71.5 0.1 constant_dynamic-slice_fusion
  71.6 4.9 %collective-permute-start.2 = (bf16[400,1024]{1,0:T(8,128)(2,1)S(1)}, bf16[400,1024]{1,0:T(8,128)(2,1)S(1)}, u32[]{:S(2)}, u32[]{:S(2)}) collective-permute-start(bf16[400,1024]{1,0:T(8,128)(2,1)S(1)} %get-tuple-element.22), channel_id=1, source_target_pairs={{256,0},{272,16},{288,32},{304,48},{320,64},{336,80},{352,96},{368... | collective-permute-start | bytes 2457608 | tf_op jit(solution)/shard_map/ppermute | solution.py:231
  76.5 0.0 copy-done
  76.5 0.1 dynamic-slice_bitcast_fusion
  76.6 0.1 copy.14.rel
  76.6 0.1 copy.12.state
  76.7 1.6 %all-to-all-done.1.pieces = f32[16,8,400]{2,1,0:T(8,128)S(1)} async-done(((f32[16,8,400]{2,1,0:T(8,128)}), f32[16,8,400]{2,1,0:T(8,128)S(1)}, u32[]{:S(2)}, u32[]{:S(2)}) %all-to-all-start.1) | async-done | bytes 204832 | tf_op jit(solution)/shard_map/all_to_all | solution.py:303
  78.3 1.0 shard_map.108
  79.3 6.1 %all-to-all-start.2 = ((f32[32,8,400]{2,1,0:T(8,128)}), f32[32,8,400]{2,1,0:T(8,128)S(1)}, u32[]{:S(2)}, u32[]{:S(2)}) async-start(f32[32,8,400]{2,1,0:T(8,128)} %shard_map.108), calls=%async_computation.2 | async-start | bytes 1048576 | tf_op jit(solution)/shard_map/all_to_all | solution.py:303
  85.5 10.5 %collective-permute-done.2.home = bf16[400,1024]{1,0:T(8,128)(2,1)S(1)} collective-permute-done((bf16[400,1024]{1,0:T(8,128)(2,1)S(1)}, bf16[400,1024]{1,0:T(8,128)(2,1)S(1)}, u32[]{:S(2)}, u32[]{:S(2)}) %collective-permute-start.2) | collective-permute-done | bytes 819232 | tf_op jit(solution)/shard_map/ppermute | solution.py:231
  95.9 0.0 copy-done.10
  96.0 4.6 %shard_map.106 = (f32[1,1024]{1,0:T(1,128)}, f32[400,1024]{1,0:T(8,128)}) custom-call(s32[1]{0:T(128)} %bitcast.block, s32[2,1024]{1,0:T(2,128)S(1)} %copy-done.7, f32[1,1024]{1,0:T(1,128)S(1)} %bitcast.15, bf16[400,1024]{1,0:T(8,128)(2,1)S(1)} %collective-permute-done.2.home, f32[400,1024]{1,0:T(8,128)} %bitcast.16, ...), custom_call_target="tpu_custom_call" | custom-call | tf_op jit(solution)/shard_map/pallas_call | solution.py:216
  100.6 4.8 %all-to-all-done.2 = f32[32,8,400]{2,1,0:T(8,128)S(1)} async-done(((f32[32,8,400]{2,1,0:T(8,128)}), f32[32,8,400]{2,1,0:T(8,128)S(1)}, u32[]{:S(2)}, u32[]{:S(2)}) %all-to-all-start.2) | async-done | bytes 409632 | tf_op jit(solution)/shard_map/all_to_all | solution.py:303
  105.3 0.9 copy.13
Async XLA Ops:
  0.6 75.8 %copy-start = (f32[256]{0:T(256)S(1)}, f32[256]{0:T(256)}, u32[]{:S(2)}) copy-start(f32[256]{0:T(256)} %param.11) | copy-start | bytes 3076
  0.6 7.4 %copy-start.9 = (s32[2,512]{1,0:T(2,128)S(1)}, s32[2,512]{1,0:T(2,128)}, u32[]{:S(2)}) copy-start(s32[2,512]{1,0:T(2,128)} %neg_a.1) | copy-start | bytes 12292
  0.7 13.7 %copy-start.8 = (s32[1024]{0:T(1024)S(1)}, s32[1024]{0:T(1024)}, u32[]{:S(2)}) copy-start(s32[1024]{0:T(1024)} %param.13) | copy-start | bytes 12292
  0.7 13.7 %copy-start.7 = (s32[2,1024]{1,0:T(2,128)S(1)}, s32[2,1024]{1,0:T(2,128)}, u32[]{:S(2)}) copy-start(s32[2,1024]{1,0:T(2,128)} %ends.7) | copy-start | bytes 24580
  3.2 23.6 %collective-permute-start = (bf16[400,1024]{1,0:T(8,128)(2,1)}, bf16[400,1024]{1,0:T(8,128)(2,1)S(1)}, u32[]{:S(2)}, u32[]{:S(2)}) collective-permute-start(bf16[400,1024]{1,0:T(8,128)(2,1)} %bitcast_convert_fusion.own), channel_id=1, source_target_pairs={{256,0},{272,16},{288,32},{304,48},{320,64},{336,80},{352,96},{368... | collective-permute-start | bytes 2457608 | tf_op jit(solution)/shard_map/ppermute | solution.py:231
  8.1 6.3 %collective-permute-start.1 = (s32[2,512]{1,0:T(2,128)S(1)}, s32[2,512]{1,0:T(2,128)S(1)}, u32[]{:S(2)}, u32[]{:S(2)}) collective-permute-start(s32[2,512]{1,0:T(2,128)S(1)} %copy-done.9), channel_id=1, source_target_pairs={{1,0},{0,1},{3,2},{2,3},{5,4},{4,5},{7,6},{6,7},{9,8},{8,9},{11,10... | collective-permute-start | bytes 12296 | tf_op jit(solution)/shard_map/ppermute | solution.py:231
  14.4 1.0 copy-start.5
  19.3 11.9 %copy-start.1 = (f32[400,1024]{1,0:T(8,128)}, f32[400,1024]{1,0:T(8,128)S(1)}, u32[]{:S(2)}) copy-start(f32[400,1024]{1,0:T(8,128)S(1)} %get-tuple-element.17.scale.scale_hbm) | copy-start | bytes 4915204
  19.3 11.9 %copy-start.2 = (f32[2,1024,128]{2,1,0:T(8,128)}, f32[2,1024,128]{2,1,0:T(8,128)S(1)}, u32[]{:S(2)}) copy-start(f32[2,1024,128]{2,1,0:T(8,128)S(1)} %get-tuple-element.18.count.count_hbm) | copy-start | bytes 3145732
  19.3 11.9 %copy-start.4 = (bf16[400,1024]{1,0:T(8,128)(2,1)}, bf16[400,1024]{1,0:T(8,128)(2,1)S(1)}, u32[]{:S(2)}) copy-start(bf16[400,1024]{1,0:T(8,128)(2,1)S(1)} %get-tuple-element.16.q.q_hbm) | copy-start | bytes 2457604
  26.7 4.5 %copy-start.3 = (bf16[400,1024]{1,0:T(8,128)(2,1)}, bf16[400,1024]{1,0:T(8,128)(2,1)S(1)}, u32[]{:S(2)}) copy-start(bf16[400,1024]{1,0:T(8,128)(2,1)S(1)} %collective-permute-done.far.far_hbm) | copy-start | bytes 2457604
  31.2 31.5 %all-to-all-start = ((f32[32,8,400]{2,1,0:T(8,128)}), f32[32,8,400]{2,1,0:T(8,128)S(1)}, u32[]{:S(2)}, u32[]{:S(2)}) async-start(f32[32,8,400]{2,1,0:T(8,128)} %bitcast.18), calls=%async_computation | async-start | bytes 1048576 | tf_op jit(solution)/shard_map/all_to_all | solution.py:303
  46.3 25.1 %copy-start.6 = (f32[256,400]{0,1:T(8,128)S(1)}, f32[256,400]{0,1:T(8,128)}, u32[]{:S(2)}) copy-start(f32[256,400]{0,1:T(8,128)} %param.10) | copy-start | bytes 1228804
  63.6 32.4 %copy-start.10 = (f32[1024]{0:T(1024)S(1)}, f32[1024]{0:T(1024)}, u32[]{:S(2)}) copy-start(f32[1024]{0:T(1024)} %param.9) | copy-start | bytes 12292
  63.6 14.8 %all-to-all-start.1 = ((f32[16,8,400]{2,1,0:T(8,128)}), f32[16,8,400]{2,1,0:T(8,128)S(1)}, u32[]{:S(2)}, u32[]{:S(2)}) async-start(f32[16,8,400]{2,1,0:T(8,128)} %shard_map.107), calls=%async_computation.1 | async-start | bytes 524288 | tf_op jit(solution)/shard_map/all_to_all | solution.py:303
  71.6 24.4 %collective-permute-start.2 = (bf16[400,1024]{1,0:T(8,128)(2,1)S(1)}, bf16[400,1024]{1,0:T(8,128)(2,1)S(1)}, u32[]{:S(2)}, u32[]{:S(2)}) collective-permute-start(bf16[400,1024]{1,0:T(8,128)(2,1)S(1)} %get-tuple-element.22), channel_id=1, source_target_pairs={{256,0},{272,16},{288,32},{304,48},{320,64},{336,80},{352,96},{368... | collective-permute-start | bytes 2457608 | tf_op jit(solution)/shard_map/ppermute | solution.py:231
  79.3 26.0 %all-to-all-start.2 = ((f32[32,8,400]{2,1,0:T(8,128)}), f32[32,8,400]{2,1,0:T(8,128)S(1)}, u32[]{:S(2)}, u32[]{:S(2)}) async-start(f32[32,8,400]{2,1,0:T(8,128)} %shard_map.108), calls=%async_computation.2 | async-start | bytes 1048576 | tf_op jit(solution)/shard_map/all_to_all | solution.py:303
